TPU v7x, 32 devices: a whole 2x2x4 slice. The times are simulated.
32 devices in a mesh: fsdp: 4 (over y, core), ctx: 8 (over z, x).
Axes of the slice: x: 2, y: 2, z: 4, core: 2. Of those that a mesh axis runs over, the one named last changes fastest.
Arguments:
- query_proj: bfloat16 [4, 1024, 4096], P('fsdp', 'ctx'), may hold values from -10 to 10
- key_proj: bfloat16 [4, 1024, 4096], P('fsdp', 'ctx'), may hold values from -10 to 10
- value_proj: bfloat16 [4, 1024, 4096], P('fsdp', 'ctx'), may hold values from -12 to 12
- modality: int32 [4, 1024], P('fsdp', 'ctx'), may hold values from 0 to 1, as said below
- out_weight: bfloat16 [2, 4096, 2048], P(None, ('fsdp', 'ctx')), may hold values from -0.09375 to 0.09375
- grad_projected: bfloat16 [4, 1024, 2048], P('fsdp', 'ctx'), may hold values from -6 to 6
Outputs:
- projected: bfloat16 [4, 1024, 2048], P('fsdp', 'ctx')
- grad_query: bfloat16 [4, 1024, 4096], P('fsdp', 'ctx')
- grad_key: bfloat16 [4, 1024, 4096], P('fsdp', 'ctx')
- grad_value: bfloat16 [4, 1024, 4096], P('fsdp', 'ctx')
Inputs may be any that keep to these rules, and one draw needn't show every extreme that they name: `modality`: each sequence holds exactly two image spans of 256 positions each, one starting within the first half and lying in the first half, the other lying in the second half; all other positions are text, so exactly half of each sequence's positions are image.
All inputs are finite; a program needn't handle non-finite values.
Results may differ from a plain program's by a relative error of at most 0.012.
The roundings to bfloat16 on the way count: a program that leaves them out, or rounds other values in their place, can miss the bound.
Values may be sent and summed in bfloat16 or wider, within the bound.
A program may use at most 320 MiB of HBM per device.

v0:
```python
import jax
import jax.numpy as jnp
from jax import lax
from jax.sharding import PartitionSpec as P

HEAD_SIZE = 128


def block_count(length):
    return max(1, min(8, length // 512))


def probabilities(query_block, key_prefix, offset):
    scaling = query_block.shape[-1] ** (-0.5)
    scores = (
        jnp.einsum("hqd,hkd->hqk", query_block, key_prefix, preferred_element_type=jnp.float32)
        * scaling
    )
    query_places = offset + jnp.arange(query_block.shape[1])
    key_places = jnp.arange(key_prefix.shape[1])
    scores = jnp.where(key_places[None, None, :] <= query_places[None, :, None], scores, -jnp.inf)
    highest = jnp.max(scores, axis=-1, keepdims=True)
    raised = jnp.exp(scores - highest)
    return raised / jnp.sum(raised, axis=-1, keepdims=True)


def attend_forward(queries, keys_all, values_all):
    length = queries.shape[1]
    block_rows = length // block_count(length)
    pieces = []
    for block_index in range(length // block_rows):
        offset = block_index * block_rows
        finish = offset + block_rows
        weights = probabilities(queries[:, offset:finish], keys_all[:, :finish], offset).astype(
            jnp.bfloat16
        )
        output = jnp.einsum(
            "hqk,hkd->hqd", weights, values_all[:, :finish], preferred_element_type=jnp.float32
        )
        pieces.append(output.astype(jnp.bfloat16))
    return jnp.concatenate(pieces, axis=1)


def attend_backward(queries, keys_all, values_all, attention, grad_attention):
    length = queries.shape[1]
    block_rows = length // block_count(length)
    scaling = queries.shape[-1] ** (-0.5)
    grad_keys = jnp.zeros(queries.shape, jnp.float32)
    grad_values = jnp.zeros(queries.shape, jnp.float32)
    query_pieces = []
    for block_index in range(length // block_rows):
        offset = block_index * block_rows
        finish = offset + block_rows
        query_block = queries[:, offset:finish]
        weights = probabilities(query_block, keys_all[:, :finish], offset)
        grad_block = grad_attention[:, offset:finish]
        attn_block = attention[:, offset:finish]
        grad_values = grad_values.at[:, :finish].add(
            jnp.einsum(
                "hqk,hqd->hkd",
                weights.astype(jnp.bfloat16),
                grad_block,
                preferred_element_type=jnp.float32,
            )
        )
        grad_weights = jnp.einsum(
            "hqd,hkd->hqk", grad_block, values_all[:, :finish], preferred_element_type=jnp.float32
        )
        row_delta = jnp.sum(
            grad_block.astype(jnp.float32) * attn_block.astype(jnp.float32), axis=-1, keepdims=True
        )
        grad_scores = (weights * (grad_weights - row_delta) * scaling).astype(jnp.bfloat16)
        query_pieces.append(
            jnp.einsum(
                "hqk,hkd->hqd",
                grad_scores,
                keys_all[:, :finish],
                preferred_element_type=jnp.float32,
            ).astype(jnp.bfloat16)
        )
        grad_keys = grad_keys.at[:, :finish].add(
            jnp.einsum("hqk,hqd->hkd", grad_scores, query_block, preferred_element_type=jnp.float32)
        )
    return (
        jnp.concatenate(query_pieces, axis=1),
        grad_keys.astype(jnp.bfloat16),
        grad_values.astype(jnp.bfloat16),
    )


def transposed_product(left, right):
    return lax.dot_general(
        left, right, (((1,), (1,)), ((), ())), preferred_element_type=jnp.float32
    )


def heads_first(flat, length, local_heads):
    return flat.reshape(length, local_heads, HEAD_SIZE).transpose(1, 0, 2)


def heads_last(stacked, length, local_width):
    return stacked.transpose(1, 0, 2).reshape(1, length, local_width)


def per_device(query_proj, key_proj, value_proj, modality, out_weight, grad_projected):
    context_size = lax.axis_size("ctx")
    row_count = query_proj.shape[1]
    inner_width = query_proj.shape[2]
    length = row_count * context_size
    local_width = inner_width // context_size
    local_heads = local_width // HEAD_SIZE
    head_query, head_key, head_value = (
        lax.all_to_all(query_proj, "ctx", split_axis=2, concat_axis=1, tiled=True),
        lax.all_to_all(key_proj, "ctx", split_axis=2, concat_axis=1, tiled=True),
        lax.all_to_all(value_proj, "ctx", split_axis=2, concat_axis=1, tiled=True),
    )
    head_query = heads_first(head_query, length, local_heads)
    head_key = heads_first(head_key, length, local_heads)
    head_value = heads_first(head_value, length, local_heads)
    attention = attend_forward(head_query, head_key, head_value)
    sending = heads_last(attention, length, local_width)
    attn_rows = lax.all_to_all(sending, "ctx", split_axis=1, concat_axis=2, tiled=True)[0]
    upstream = grad_projected[0]
    weight_piece = lax.all_gather(out_weight, ("fsdp", "ctx"), axis=1, tiled=True)
    text_out = jnp.dot(attn_rows, weight_piece[0], preferred_element_type=jnp.float32)
    image_out = jnp.dot(attn_rows, weight_piece[1], preferred_element_type=jnp.float32)
    text_grad = transposed_product(upstream, weight_piece[0])
    image_grad = transposed_product(upstream, weight_piece[1])
    text_out, image_out, text_grad, image_grad = (text_out, image_out, text_grad, image_grad)
    image_rows = (modality[0] == 1)[:, None]
    projected = jnp.where(image_rows, image_out, text_out).astype(jnp.bfloat16)[None]
    grad_rows = jnp.where(image_rows, image_grad, text_grad).astype(jnp.bfloat16)
    grad_heads = lax.all_to_all(grad_rows[None], "ctx", split_axis=2, concat_axis=1, tiled=True)
    grad_heads = heads_first(grad_heads, length, local_heads)
    grad_q, grad_k, grad_v = attend_backward(
        head_query, head_key, head_value, attention, grad_heads
    )
    grad_query, grad_key, grad_value = (
        lax.all_to_all(
            heads_last(grad_q, length, local_width), "ctx", split_axis=1, concat_axis=2, tiled=True
        ),
        lax.all_to_all(
            heads_last(grad_k, length, local_width), "ctx", split_axis=1, concat_axis=2, tiled=True
        ),
        lax.all_to_all(
            heads_last(grad_v, length, local_width), "ctx", split_axis=1, concat_axis=2, tiled=True
        ),
    )
    return (projected, grad_query, grad_key, grad_value)


def solution(mesh):
    placed = (
        P("fsdp", "ctx", None),
        P("fsdp", "ctx", None),
        P("fsdp", "ctx", None),
        P("fsdp", "ctx"),
        P(None, ("fsdp", "ctx"), None),
        P("fsdp", "ctx", None),
    )
    return jax.shard_map(
        per_device,
        mesh=mesh,
        in_specs=placed,
        out_specs=(
            P("fsdp", "ctx", None),
            P("fsdp", "ctx", None),
            P("fsdp", "ctx", None),
            P("fsdp", "ctx", None),
        ),
        check_vma=False,
    )
```

profile of v0, /device:TPU:0, one launch (start us, length us, event | category | flops | bytes accessed | tf_op | source)
XLA Modules:
  0.0 543.5 jit_solution(6970841541703421704)
XLA Ops:
  7.9 5.0 copy.130
  13.5 23.4 %reduce.8 = bf16[4096,128]{1,0:T(8,128)(2,1)} reduce(bf16[4096,1,128]{2,1,0:T(2,128)(2,1)S(1)} %bitcast.141, bf16[]{:T(256)} %broadcast.182), dimensions={1}, to_apply=%bitcast.103.reduce_sub_computation | reduce | bytes 2097154
  36.8 2.1 reshape.224
  39.0 7.3 %all-to-all-start = ((bf16[8,2,32768]{2,1,0:T(2,128)(2,1)}), bf16[8,2,32768]{2,1,0:T(2,128)(2,1)}, u32[]{:S(2)}, u32[]{:S(2)}) async-start(bf16[8,2,32768]{2,1,0:T(2,128)(2,1)} %reshape.224), calls=%async_computation | async-start | bytes 2097152 | tf_op jit(solution)/shard_map/all_to_all | solution.py:113
  46.2 5.0 copy.133
  51.3 23.4 %reduce.9 = bf16[4096,128]{1,0:T(8,128)(2,1)} reduce(bf16[4096,1,128]{2,1,0:T(2,128)(2,1)S(1)} %bitcast.147, bf16[]{:T(256)} %broadcast.182), dimensions={1}, to_apply=%bitcast.105.reduce_sub_computation | reduce | bytes 2097154
  74.6 2.1 reshape.226
  76.8 16.4 %all-to-all-done = bf16[8,2,32768]{2,1,0:T(2,128)(2,1)} async-done(((bf16[8,2,32768]{2,1,0:T(2,128)(2,1)}), bf16[8,2,32768]{2,1,0:T(2,128)(2,1)}, u32[]{:S(2)}, u32[]{:S(2)}) %all-to-all-start) | async-done | bytes 1048608 | tf_op jit(solution)/shard_map/all_to_all | solution.py:113
  93.2 7.5 %all-to-all-start.1 = ((bf16[8,2,32768]{2,1,0:T(2,128)(2,1)}), bf16[8,2,32768]{2,1,0:T(2,128)(2,1)}, u32[]{:S(2)}, u32[]{:S(2)}) async-start(bf16[8,2,32768]{2,1,0:T(2,128)(2,1)} %reshape.226), calls=%async_computation.1 | async-start | bytes 2097152 | tf_op jit(solution)/shard_map/all_to_all | solution.py:114
  100.7 5.0 copy.136
  105.7 23.4 %reduce.10 = bf16[4096,128]{1,0:T(8,128)(2,1)} reduce(bf16[4096,1,128]{2,1,0:T(2,128)(2,1)S(1)} %bitcast.148, bf16[]{:T(256)} %broadcast.182), dimensions={1}, to_apply=%bitcast.107.reduce_sub_computation | reduce | bytes 2097154
  129.1 2.1 reshape.228
  131.7 4.3 reshape.225
  139.9 5.2 all-to-all-start.2
  145.1 4.4 reshape.227
  153.3 5.2 fusion.58
  158.5 103.3 %all-gather.2.cloned.1.call-done = bf16[2,4096,2048]{2,1,0:T(8,128)(2,1)} async-done(((bf16[2,128,2048]{2,1,0:T(8,128)(2,1)}), bf16[2,4096,2048]{2,1,0:T(8,128)(2,1)}) %all-gather.2.cloned.1.call-update) | async-done | bytes 33554448 | tf_op jit(solution)/shard_map/all_gather | solution.py:124
  261.9 11.4 %fusion.2 = bf16[128,4096]{1,0:T(8,128)(2,1)S(1)} fusion(bf16[2,4096,2048]{2,1,0:T(8,128)(2,1)} %all-gather.2.cloned.1.call-done, bf16[1,128,2048]{2,1,0:T(8,128)(2,1)S(1)} %copy-done), kind=kOutput, calls=%fused_computation.4 | convolution fusion | flops 2147483648 | bytes 18350080 | tf_op jit(solution)/shard_map/dot_general | solution.py:92
  273.2 12.3 %fusion.9 = bf16[1,128,4096]{2,1,0:T(8,128)(2,1)} fusion(bf16[128,4096]{1,0:T(8,128)(2,1)S(1)} %fusion.2, bf16[2,4096,2048]{2,1,0:T(8,128)(2,1)} %all-gather.2.cloned.1.call-done, pred[128]{0:T(512)(128)(4,1)S(1)} %compare_bitcast_fusion, bf16[1,128,2048]{2,1,0:T(8,128)(2,1)S(1)} %copy-done), kind=kOutput, calls=%fused_computation.14 | convolution fusion | flops 2148007936 | bytes 19398784 | tf_op jit(solution)/shard_map/dot_general | solution.py:92
  285.6 5.0 copy.143
  290.6 23.5 %reduce.11 = bf16[4096,128]{1,0:T(8,128)(2,1)} reduce(bf16[4096,1,128]{2,1,0:T(2,128)(2,1)S(1)} %bitcast.143, bf16[]{:T(256)} %broadcast.182), dimensions={1}, to_apply=%bitcast.111.reduce_sub_computation | reduce | bytes 2097154
  314.2 2.1 reshape.232
  316.3 4.2 all-to-all-start.4
  320.6 5.3 fusion.13
  325.9 4.3 reshape.229
  332.0 2.3 reshape.218
  334.3 2.3 copy.138
  340.3 2.1 fusion.67
  345.1 2.0 all-to-all-done.4
  347.0 5.8 %reshape.233 = bf16[4096,1,128]{2,1,0:T(2,128)(2,1)} reshape(bf16[8,2,32768]{2,1,0:T(2,128)(2,1)} %all-to-all-done.4) | data formatting | bytes 2097152
  356.2 2.3 reshape.220
  358.5 2.3 copy.145
  360.7 2.7 multiply_reduce_fusion.1
  363.5 2.0 multiply_convert_fusion.1
  366.6 2.3 copy.140
  368.9 6.1 %copy.141 = bf16[1,1024,512]{2,0,1:T(2,128)(2,1)} copy(bf16[1,1024,512]{1,2,0:T(8,128)(2,1)} %bitcast.157) | data formatting | bytes 2097152 | tf_op jit(solution)/shard_map/reshape | solution.py:102
  375.0 9.0 %reduce.12 = bf16[1024,512]{1,0:T(8,128)(2,1)} reduce(bf16[1024,1,512]{2,1,0:T(2,128)(2,1)} %bitcast.144, bf16[]{:T(256)} %broadcast.182), dimensions={1}, to_apply=%bitcast.109.reduce_sub_computation | reduce | bytes 2097154
  384.1 2.6 reshape.230
  386.7 4.6 all-to-all-start.3
  393.2 5.5 %multiply_convert_fusion = bf16[4,512,1024]{2,1,0:T(8,128)(2,1)S(1)} fusion(f32[4,512]{1,0:T(4,128)S(1)} %get-tuple-element.85, f32[4,512,1024]{2,1,0:T(8,128)} %get-tuple-element.87, f32[4,512]{1,0:T(4,128)S(1)} %get-tuple-element.86, bf16[4,1024,128]{2,1,0:T(8,128)(2,1)} %bitcast.172, bf16[1024,4,128]{2,0,1:T(8,128)(2,1)} %copy.138), kind=kOutput, calls=%fused_computation.8 | convolution fusion | flops 547356672 | bytes 14172160 | tf_op jit(solution)/shard_map/hqd,hkd->hqk/dot_general | solution.py:66
  398.7 2.2 add_convert_fusion.1
  401.0 6.0 %copy.154 = bf16[1,1024,512]{2,0,1:T(2,128)(2,1)} copy(bf16[1,1024,512]{1,2,0:T(8,128)(2,1)} %bitcast.166) | data formatting | bytes 2097152 | tf_op jit(solution)/shard_map/reshape | solution.py:102
  407.0 9.0 %reduce.14 = bf16[1024,512]{1,0:T(8,128)(2,1)} reduce(bf16[1024,1,512]{2,1,0:T(2,128)(2,1)} %bitcast.145, bf16[]{:T(256)} %broadcast.182), dimensions={1}, to_apply=%bitcast.115.reduce_sub_computation | reduce | bytes 2097154
  416.0 2.6 reshape.236
  418.6 6.2 %all-to-all-start.6 = ((bf16[8,2,32768]{2,1,0:T(2,128)(2,1)}), bf16[8,2,32768]{2,1,0:T(2,128)(2,1)}, u32[]{:S(2)}, u32[]{:S(2)}) async-start(bf16[8,2,32768]{2,1,0:T(2,128)(2,1)} %reshape.236), calls=%async_computation.6 | async-start | bytes 2097152 | tf_op jit(solution)/shard_map/all_to_all | solution.py:142
  426.7 3.7 convolution_convert_fusion
  431.1 3.9 copy.149
  435.0 9.2 %reduce.13 = bf16[1024,512]{1,0:T(8,128)(2,1)} reduce(bf16[1024,1,512]{2,1,0:T(2,128)(2,1)} %bitcast.146, bf16[]{:T(256)} %broadcast.182), dimensions={1}, to_apply=%bitcast.113.reduce_sub_computation | reduce | bytes 2097154
  444.2 2.6 reshape.234
  446.8 3.6 all-to-all-done.6
  450.3 4.5 all-to-all-start.5
  456.7 4.1 add_convert_fusion
  460.8 4.6 copy.159
  465.4 8.0 %reduce.15 = bf16[1024,512]{1,0:T(8,128)(2,1)} reduce(bf16[1024,1,512]{2,1,0:T(2,128)(2,1)S(1)} %bitcast.142, bf16[]{:T(256)} %broadcast.182), dimensions={1}, to_apply=%bitcast.117.reduce_sub_computation | reduce | bytes 2097154
  473.4 2.6 reshape.238
  476.0 4.2 all-to-all-done.5
  480.2 4.5 all-to-all-start.7
  484.7 4.3 reshape.231
  490.3 2.3 copy.142
  492.5 4.3 reshape.237
  501.0 4.3 reshape.235
  510.1 4.3 reshape.239
  518.6 8.5 %fusion.3 = bf16[128,2048]{1,0:T(8,128)(2,1)S(1)} fusion(bf16[128,4096]{0,1:T(8,128)(2,1)} %bitcast.177, bf16[2,4096,2048]{2,1,0:T(8,128)(2,1)} %all-gather.2.cloned.1.call-done), kind=kOutput, calls=%fused_computation.5 | convolution fusion | flops 2147483648 | bytes 18350080 | tf_op jit(solution)/shard_map/dot_general | solution.py:126
  527.2 9.0 %fusion.17 = bf16[1,128,2048]{2,1,0:T(8,128)(2,1)} fusion(bf16[128,2048]{1,0:T(8,128)(2,1)S(1)} %fusion.3, bf16[128,4096]{0,1:T(8,128)(2,1)S(1)} %bitcast.178, bf16[2,4096,2048]{2,1,0:T(8,128)(2,1)} %all-gather.2.cloned.1.call-done, pred[128]{0:T(512)(128)(4,1)S(1)} %compare_bitcast_fusion), kind=kOutput, calls=%fused_computation.26 | convolution fusion | flops 2147745792 | bytes 18874496 | tf_op jit(solution)/shard_map/dot_general | solution.py:125
  (74 shorter events, 42.5 us)
Async XLA Ops:
  7.2 254.7 %copy-start = (bf16[1,128,2048]{2,1,0:T(8,128)(2,1)S(1)}, bf16[1,128,2048]{2,1,0:T(8,128)(2,1)}, u32[]{:S(2)}) copy-start(bf16[1,128,2048]{2,1,0:T(8,128)(2,1)} %param.23) | copy-start | bytes 1572868
  7.2 254.7 %all-gather.2.cloned.1.call-start = ((), (), s32[]{:S(2)}) async-start(), calls=%async_computation.8 | async-start | bytes 34603008 | tf_op jit(solution)/shard_map/all_gather | solution.py:124
  39.0 54.2 %all-to-all-start = ((bf16[8,2,32768]{2,1,0:T(2,128)(2,1)}), bf16[8,2,32768]{2,1,0:T(2,128)(2,1)}, u32[]{:S(2)}, u32[]{:S(2)}) async-start(bf16[8,2,32768]{2,1,0:T(2,128)(2,1)} %reshape.224), calls=%async_computation | async-start | bytes 2097152 | tf_op jit(solution)/shard_map/all_to_all | solution.py:113
  93.2 46.7 %all-to-all-start.1 = ((bf16[8,2,32768]{2,1,0:T(2,128)(2,1)}), bf16[8,2,32768]{2,1,0:T(2,128)(2,1)}, u32[]{:S(2)}, u32[]{:S(2)}) async-start(bf16[8,2,32768]{2,1,0:T(2,128)(2,1)} %reshape.226), calls=%async_computation.1 | async-start | bytes 2097152 | tf_op jit(solution)/shard_map/all_to_all | solution.py:114
  100.6 30.7 %copy-start.15 = (s32[1,128]{1,0:T(1,128)S(1)}, s32[1,128]{1,0:T(1,128)}, u32[]{:S(2)}) copy-start(s32[1,128]{1,0:T(1,128)} %param.21) | copy-start | bytes 1540
  139.9 176.4 %all-to-all-start.2 = ((bf16[8,2,32768]{2,1,0:T(2,128)(2,1)}), bf16[8,2,32768]{2,1,0:T(2,128)(2,1)}, u32[]{:S(2)}, u32[]{:S(2)}) async-start(bf16[8,2,32768]{2,1,0:T(2,128)(2,1)} %reshape.228), calls=%async_computation.2 | async-start | bytes 2097152 | tf_op jit(solution)/shard_map/all_to_all | solution.py:115
  149.7 3.6 copy-start.5
  153.3 5.3 copy-start.10
  316.3 30.7 %all-to-all-start.4 = ((bf16[8,2,32768]{2,1,0:T(2,128)(2,1)}), bf16[8,2,32768]{2,1,0:T(2,128)(2,1)}, u32[]{:S(2)}, u32[]{:S(2)}) async-start(bf16[8,2,32768]{2,1,0:T(2,128)(2,1)} %reshape.232), calls=%async_computation.4 | async-start | bytes 2097152 | tf_op jit(solution)/shard_map/all_to_all | solution.py:133
  330.4 6.2 %copy-start.6 = (bf16[1024,4,128]{2,0,1:T(8,128)(2,1)S(1)}, bf16[1024,4,128]{2,0,1:T(8,128)(2,1)}, u32[]{:S(2)}) copy-start(bf16[1024,4,128]{2,0,1:T(8,128)(2,1)} %copy.132) | copy-start | bytes 3145732
  330.4 6.2 %copy-start.11 = (bf16[1024,4,128]{2,0,1:T(8,128)(2,1)S(1)}, bf16[1024,4,128]{2,0,1:T(8,128)(2,1)}, u32[]{:S(2)}) copy-start(bf16[1024,4,128]{2,0,1:T(8,128)(2,1)} %copy-done.10) | copy-start | bytes 3145732
  336.6 2.2 copy-start.2
  336.6 2.5 copy-start.13
  342.5 1.9 copy-start.8
  345.1 15.7 %copy-start.3 = (bf16[4,512,512]{1,2,0:T(8,128)(2,1)}, bf16[4,512,512]{1,2,0:T(8,128)(2,1)S(1)}, u32[]{:S(2)}) copy-start(bf16[4,512,512]{1,2,0:T(8,128)(2,1)S(1)} %fusion.21) | copy-start | bytes 6291460
  360.7 2.8 copy-start.9
  386.7 31.9 %all-to-all-start.3 = ((bf16[8,2,32768]{2,1,0:T(2,128)(2,1)}), bf16[8,2,32768]{2,1,0:T(2,128)(2,1)}, u32[]{:S(2)}, u32[]{:S(2)}) async-start(bf16[8,2,32768]{2,1,0:T(2,128)(2,1)} %reshape.230), calls=%async_computation.3 | async-start | bytes 2097152 | tf_op jit(solution)/shard_map/all_to_all | solution.py:122
  393.2 5.5 %copy-start.7 = (bf16[1024,4,128]{2,0,1:T(8,128)(2,1)S(1)}, bf16[1024,4,128]{2,0,1:T(8,128)(2,1)}, u32[]{:S(2)}) copy-start(bf16[1024,4,128]{2,0,1:T(8,128)(2,1)} %copy.132) | copy-start | bytes 3145732
  398.7 2.3 copy-start.12
  418.6 31.8 %all-to-all-start.6 = ((bf16[8,2,32768]{2,1,0:T(2,128)(2,1)}), bf16[8,2,32768]{2,1,0:T(2,128)(2,1)}, u32[]{:S(2)}, u32[]{:S(2)}) async-start(bf16[8,2,32768]{2,1,0:T(2,128)(2,1)} %reshape.236), calls=%async_computation.6 | async-start | bytes 2097152 | tf_op jit(solution)/shard_map/all_to_all | solution.py:142
  435.0 19.8 %copy-start.4 = (bf16[4,512,512]{1,2,0:T(8,128)(2,1)S(1)}, bf16[4,512,512]{1,2,0:T(8,128)(2,1)}, u32[]{:S(2)}) copy-start(bf16[4,512,512]{1,2,0:T(8,128)(2,1)} %copy-done.3) | copy-start | bytes 6291460
  450.3 29.9 %all-to-all-start.5 = ((bf16[8,2,32768]{2,1,0:T(2,128)(2,1)}), bf16[8,2,32768]{2,1,0:T(2,128)(2,1)}, u32[]{:S(2)}, u32[]{:S(2)}) async-start(bf16[8,2,32768]{2,1,0:T(2,128)(2,1)} %reshape.234), calls=%async_computation.5 | async-start | bytes 2097152 | tf_op jit(solution)/shard_map/all_to_all | solution.py:139
  480.2 29.9 %all-to-all-start.7 = ((bf16[8,2,32768]{2,1,0:T(2,128)(2,1)}), bf16[8,2,32768]{2,1,0:T(2,128)(2,1)}, u32[]{:S(2)}, u32[]{:S(2)}) async-start(bf16[8,2,32768]{2,1,0:T(2,128)(2,1)} %reshape.238), calls=%async_computation.7 | async-start | bytes 2097152 | tf_op jit(solution)/shard_map/all_to_all | solution.py:145
  518.6 8.5 %copy-start.14 = (bf16[1,128,8,512]{1,3,2,0:T(8,128)(2,1)S(1)}, bf16[1,128,8,512]{1,3,2,0:T(8,128)(2,1)}, u32[]{:S(2)}) copy-start(bf16[1,128,8,512]{1,3,2,0:T(8,128)(2,1)} %copy.142) | copy-start | bytes 3145732
  527.2 9.1 %copy-start.1 = (bf16[1,128,2048]{2,1,0:T(8,128)(2,1)S(1)}, bf16[1,128,2048]{2,1,0:T(8,128)(2,1)}, u32[]{:S(2)}) copy-start(bf16[1,128,2048]{2,1,0:T(8,128)(2,1)} %param.23) | copy-start | bytes 1572868
Sparse Core Ops, SparseCore 0:
  11.0 250.7 all-gather.1
where the time goes:
time: 554 us; the launch traced here: 544 us
  local copies, waits for them, and re-layouts  140 us (25%)
  other arithmetic  139 us (25%)
  waiting for transfers between devices  132 us (24%)
  matrix products  74.5 us (13%)
  starting transfers between devices  44 us (8%)
  between operations  15 us (3%)
    unnamed x8, other arithmetic  129 us
    all_gather x1, waiting for transfers between devices, per_device(): lax.all_gather(out_weight, ('fsdp', 'ctx'), axis=1, tiled=True)  103 us
    unnamed x63, local copies, waits for them, and re-layouts  85.6 us
    dot_general x2, matrix products, transposed_product(): lax.dot_general(left, right, (((1,), (1,)), ((), ())), preferred_element_...  23.7 us
    reshape x4, local copies, waits for them, and re-layouts, heads_last(): return stacked.transpose(1, 0, 2).reshape(1, length, local_width)  20.6 us
    all_to_all x1, waiting for transfers between devices, per_device(): lax.all_to_all(query_proj, 'ctx', split_axis=2, concat_axis=1, tiled=True)  16.4 us
    reshape x8, local copies, waits for them, and re-layouts, heads_first(): return flat.reshape(length, local_heads, HEAD_SIZE).transpose(1, 0, 2)  13.8 us
  transfers between devices with their start and end apart: 9, of which 7 were waited for; matrix products, arithmetic and copies ran while one was open for 52% of the time, Pallas kernels for 0%

commit v1 on v0

--- a/solution.py
+++ b/solution.py
@@ -121,7 +121,10 @@
     sending = heads_last(attention, length, local_width)
     attn_rows = lax.all_to_all(sending, "ctx", split_axis=1, concat_axis=2, tiled=True)[0]
     upstream = grad_projected[0]
-    weight_piece = lax.all_gather(out_weight, ("fsdp", "ctx"), axis=1, tiled=True)
+    arrange_the_weights = lambda mine_x, dim_at: jnp.concatenate(
+        jax.lax.all_gather(mine_x, ("fsdp", "ctx")), axis=dim_at
+    )
+    weight_piece = arrange_the_weights(out_weight, 1)
     text_out = jnp.dot(attn_rows, weight_piece[0], preferred_element_type=jnp.float32)
     image_out = jnp.dot(attn_rows, weight_piece[1], preferred_element_type=jnp.float32)
     text_grad = transposed_product(upstream, weight_piece[0])

time: 554 us -> 579 us (1.045)
  local copies, waits for them, and re-layouts: 140 us -> 168 us
    slice x0 -> x1, local copies, waits for them, and re-layouts: none -> 23.6 us  [per_device(): weight_piece[0]]
    unnamed x63 -> x61, local copies, waits for them, and re-layouts: 85.6 us -> 91.8 us
  transfers between devices with their start and end apart: 9 -> 9, of which waited for: 7 -> 5; matrix products, arithmetic and copies ran while one was open for 52% -> 58% of each run, Pallas kernels for 0% -> 0%
where the time goes in v1:
time: 579 us; the launch traced here: 568 us
  local copies, waits for them, and re-layouts  168 us (29%)
  other arithmetic  139 us (24%)
  waiting for transfers between devices  127 us (22%)
  matrix products  73.9 us (13%)
  starting transfers between devices  46 us (8%)
  between operations  15 us (3%)
    unnamed x8, other arithmetic  129 us
    all_gather x1, waiting for transfers between devices, per_device(): jax.lax.all_gather(mine_x, ('fsdp', 'ctx'))  103 us
    unnamed x61, local copies, waits for them, and re-layouts  91.8 us
    dot_general x2, matrix products, transposed_product(): lax.dot_general(left, right, (((1,), (1,)), ((), ())), preferred_element_...  23.7 us
    slice x1, local copies, waits for them, and re-layouts, per_device(): weight_piece[0]  23.6 us
    reshape x4, local copies, waits for them, and re-layouts, heads_last(): return stacked.transpose(1, 0, 2).reshape(1, length, local_width)  20.7 us
    all_to_all x1, waiting for transfers between devices, per_device(): lax.all_to_all(query_proj, 'ctx', split_axis=2, concat_axis=1, tiled=True)  16.3 us
    reshape x8, local copies, waits for them, and re-layouts, heads_first(): return flat.reshape(length, local_heads, HEAD_SIZE).transpose(1, 0, 2)  13.8 us
  transfers between devices with their start and end apart: 9, of which 5 were waited for; matrix products, arithmetic and copies ran while one was open for 58% of the time, Pallas kernels for 0%

profile of v1, /device:TPU:0, one launch (start us, length us, event | category | flops | bytes accessed | tf_op | source)
XLA Modules:
  0.0 568.4 jit_solution(203485944951900923)
XLA Ops:
  7.9 5.0 copy.130
  13.5 23.4 %reduce.8 = bf16[4096,128]{1,0:T(8,128)(2,1)} reduce(bf16[4096,1,128]{2,1,0:T(2,128)(2,1)S(1)} %bitcast.137, bf16[]{:T(256)} %broadcast.182), dimensions={1}, to_apply=%bitcast.88.reduce_sub_computation | reduce | bytes 2097154
  36.8 2.1 reshape.234
  39.0 7.3 %all-to-all-start = ((bf16[8,2,32768]{2,1,0:T(2,128)(2,1)}), bf16[8,2,32768]{2,1,0:T(2,128)(2,1)}, u32[]{:S(2)}, u32[]{:S(2)}) async-start(bf16[8,2,32768]{2,1,0:T(2,128)(2,1)} %reshape.234), calls=%async_computation | async-start | bytes 2097152 | tf_op jit(solution)/shard_map/all_to_all | solution.py:113
  46.2 5.0 copy.133
  51.3 23.4 %reduce.9 = bf16[4096,128]{1,0:T(8,128)(2,1)} reduce(bf16[4096,1,128]{2,1,0:T(2,128)(2,1)S(1)} %bitcast.143, bf16[]{:T(256)} %broadcast.182), dimensions={1}, to_apply=%bitcast.90.reduce_sub_computation | reduce | bytes 2097154
  74.6 2.1 reshape.236
  76.8 16.3 %all-to-all-done = bf16[8,2,32768]{2,1,0:T(2,128)(2,1)} async-done(((bf16[8,2,32768]{2,1,0:T(2,128)(2,1)}), bf16[8,2,32768]{2,1,0:T(2,128)(2,1)}, u32[]{:S(2)}, u32[]{:S(2)}) %all-to-all-start) | async-done | bytes 1048608 | tf_op jit(solution)/shard_map/all_to_all | solution.py:113
  93.1 7.5 %all-to-all-start.1 = ((bf16[8,2,32768]{2,1,0:T(2,128)(2,1)}), bf16[8,2,32768]{2,1,0:T(2,128)(2,1)}, u32[]{:S(2)}, u32[]{:S(2)}) async-start(bf16[8,2,32768]{2,1,0:T(2,128)(2,1)} %reshape.236), calls=%async_computation.1 | async-start | bytes 2097152 | tf_op jit(solution)/shard_map/all_to_all | solution.py:114
  100.6 5.0 copy.136
  105.7 23.4 %reduce.10 = bf16[4096,128]{1,0:T(8,128)(2,1)} reduce(bf16[4096,1,128]{2,1,0:T(2,128)(2,1)S(1)} %bitcast.144, bf16[]{:T(256)} %broadcast.182), dimensions={1}, to_apply=%bitcast.92.reduce_sub_computation | reduce | bytes 2097154
  129.0 2.1 reshape.238
  131.7 4.3 reshape.235
  139.8 5.3 all-to-all-start.2
  145.1 4.4 reshape.237
  153.2 5.2 fusion.54
  158.4 103.3 %all-gather.3.cloned.1.call-done = bf16[64,128,2048]{2,1,0:T(8,128)(2,1)} async-done(((bf16[2,128,2048]{2,1,0:T(8,128)(2,1)}), bf16[64,128,2048]{2,1,0:T(8,128)(2,1)}) %all-gather.3.cloned.1.call-update) | async-done | bytes 33554448 | tf_op jit(solution)/shard_map/all_gather | solution.py:125
  261.7 23.6 %fusion.53 = (bf16[1,32,128,2048]{3,2,0,1:T(8,128)(2,1)}, bf16[1,32,128,2048]{3,2,0,1:T(8,128)(2,1)}) fusion(bf16[2,32,128,2048]{3,2,0,1:T(8,128)(2,1)} %bitcast.126), kind=kLoop, calls=%fused_computation.70 | loop fusion | bytes 67108864 | tf_op jit(solution)/shard_map/slice | solution.py:128
  285.3 11.4 %fusion.19 = bf16[128,4096]{1,0:T(8,128)(2,1)S(1)} fusion(bf16[4096,2048]{1,0:T(8,128)(2,1)} %bitcast.122, bf16[1,128,2048]{2,1,0:T(8,128)(2,1)S(1)} %copy-done), kind=kOutput, calls=%fused_computation.40 | convolution fusion | flops 2147483648 | bytes 18350080 | tf_op jit(solution)/shard_map/dot_general | solution.py:92
  296.7 12.4 %fusion.4 = bf16[1,128,4096]{2,1,0:T(8,128)(2,1)} fusion(bf16[128,4096]{1,0:T(8,128)(2,1)S(1)} %fusion.19, bf16[4096,2048]{1,0:T(8,128)(2,1)} %bitcast.124, pred[128]{0:T(512)(128)(4,1)S(1)} %compare_bitcast_fusion, bf16[1,128,2048]{2,1,0:T(8,128)(2,1)S(1)} %copy-done), kind=kOutput, calls=%fused_computation.8 | convolution fusion | flops 2148007936 | bytes 19398784 | tf_op jit(solution)/shard_map/dot_general | solution.py:92
  309.1 5.0 copy.143
  314.1 23.5 %reduce.11 = bf16[4096,128]{1,0:T(8,128)(2,1)} reduce(bf16[4096,1,128]{2,1,0:T(2,128)(2,1)S(1)} %bitcast.139, bf16[]{:T(256)} %broadcast.182), dimensions={1}, to_apply=%bitcast.96.reduce_sub_computation | reduce | bytes 2097154
  337.6 2.1 reshape.242
  339.8 4.2 all-to-all-start.4
  344.0 5.3 fusion.8
  349.4 4.3 reshape.239
  355.5 2.3 reshape.226
  357.8 2.3 copy.138
  363.8 2.1 fusion.63
  370.5 5.8 %reshape.243 = bf16[4096,1,128]{2,1,0:T(2,128)(2,1)} reshape(bf16[8,2,32768]{2,1,0:T(2,128)(2,1)} %all-to-all-done.4) | data formatting | bytes 2097152
  379.7 2.3 reshape.229
  382.0 2.3 copy.145
  384.2 2.7 multiply_reduce_fusion.1
  387.0 2.0 multiply_convert_fusion.1
  390.1 2.3 copy.140
  392.4 6.1 %copy.141 = bf16[1,1024,512]{2,0,1:T(2,128)(2,1)} copy(bf16[1,1024,512]{1,2,0:T(8,128)(2,1)} %bitcast.153) | data formatting | bytes 2097152 | tf_op jit(solution)/shard_map/reshape | solution.py:102
  398.5 9.0 %reduce.12 = bf16[1024,512]{1,0:T(8,128)(2,1)} reduce(bf16[1024,1,512]{2,1,0:T(2,128)(2,1)} %bitcast.140, bf16[]{:T(256)} %broadcast.182), dimensions={1}, to_apply=%bitcast.94.reduce_sub_computation | reduce | bytes 2097154
  407.6 2.6 reshape.240
  410.2 4.7 all-to-all-start.3
  416.7 5.5 multiply_convert_fusion
  422.2 2.2 add_convert_fusion.1
  424.5 6.0 %copy.154 = bf16[1,1024,512]{2,0,1:T(2,128)(2,1)} copy(bf16[1,1024,512]{1,2,0:T(8,128)(2,1)} %bitcast.162) | data formatting | bytes 2097152 | tf_op jit(solution)/shard_map/reshape | solution.py:102
  430.5 9.0 %reduce.14 = bf16[1024,512]{1,0:T(8,128)(2,1)} reduce(bf16[1024,1,512]{2,1,0:T(2,128)(2,1)} %bitcast.141, bf16[]{:T(256)} %broadcast.182), dimensions={1}, to_apply=%bitcast.100.reduce_sub_computation | reduce | bytes 2097154
  439.5 2.6 reshape.246
  442.1 6.2 %all-to-all-start.6 = ((bf16[8,2,32768]{2,1,0:T(2,128)(2,1)}), bf16[8,2,32768]{2,1,0:T(2,128)(2,1)}, u32[]{:S(2)}, u32[]{:S(2)}) async-start(bf16[8,2,32768]{2,1,0:T(2,128)(2,1)} %reshape.246), calls=%async_computation.6 | async-start | bytes 2097152 | tf_op jit(solution)/shard_map/all_to_all | solution.py:145
  450.3 3.7 convolution_convert_fusion
  454.6 3.9 copy.149
  458.6 9.2 %reduce.13 = bf16[1024,512]{1,0:T(8,128)(2,1)} reduce(bf16[1024,1,512]{2,1,0:T(2,128)(2,1)} %bitcast.142, bf16[]{:T(256)} %broadcast.182), dimensions={1}, to_apply=%bitcast.98.reduce_sub_computation | reduce | bytes 2097154
  467.7 2.6 reshape.244
  470.4 3.5 all-to-all-done.6
  473.9 4.4 all-to-all-start.5
  480.2 4.1 add_convert_fusion
  484.3 4.6 copy.159
  489.0 8.0 %reduce.15 = bf16[1024,512]{1,0:T(8,128)(2,1)} reduce(bf16[1024,1,512]{2,1,0:T(2,128)(2,1)S(1)} %bitcast.138, bf16[]{:T(256)} %broadcast.182), dimensions={1}, to_apply=%bitcast.102.reduce_sub_computation | reduce | bytes 2097154
  497.0 2.6 reshape.248
  499.6 4.3 reshape.241
  506.8 5.8 %reshape.247 = bf16[1024,1,512]{2,1,0:T(2,128)(2,1)} reshape(bf16[8,2,32768]{2,1,0:T(2,128)(2,1)} %all-to-all-done.6) | data formatting | bytes 2097152
  515.8 2.3 copy.162
  518.0 6.3 %all-to-all-start.7 = ((bf16[8,2,32768]{2,1,0:T(2,128)(2,1)}), bf16[8,2,32768]{2,1,0:T(2,128)(2,1)}, u32[]{:S(2)}, u32[]{:S(2)}) async-start(bf16[8,2,32768]{2,1,0:T(2,128)(2,1)} %reshape.248), calls=%async_computation.7 | async-start | bytes 2097152 | tf_op jit(solution)/shard_map/all_to_all | solution.py:148
  524.3 5.8 %reshape.245 = bf16[1024,1,512]{2,1,0:T(2,128)(2,1)} reshape(bf16[8,2,32768]{2,1,0:T(2,128)(2,1)} %all-to-all-done.5) | data formatting | bytes 2097152
  533.3 2.3 copy.161
  535.5 8.1 %fusion.64 = bf16[128,2048]{1,0:T(8,128)(2,1)S(1)} fusion(bf16[128,4096]{0,1:T(8,128)(2,1)S(1)} %bitcast.127, bf16[4096,2048]{1,0:T(8,128)(2,1)} %bitcast.123), kind=kOutput, calls=%fused_computation.73 | convolution fusion | flops 2147483648 | bytes 18350080 | tf_op jit(solution)/shard_map/dot_general | solution.py:129
  543.7 8.9 %fusion.11 = bf16[1,128,2048]{2,1,0:T(8,128)(2,1)} fusion(bf16[128,2048]{1,0:T(8,128)(2,1)S(1)} %fusion.64, bf16[128,4096]{0,1:T(8,128)(2,1)S(1)} %bitcast.128, bf16[4096,2048]{1,0:T(8,128)(2,1)} %bitcast.125, pred[128]{0:T(512)(128)(4,1)S(1)} %compare_bitcast_fusion), kind=kOutput, calls=%fused_computation.20 | convolution fusion | flops 2147745792 | bytes 18874496 | tf_op jit(solution)/shard_map/dot_general | solution.py:128
  552.6 4.4 reshape.249
  (73 shorter events, 43.4 us)
Async XLA Ops:
  7.2 278.2 %copy-start = (bf16[1,128,2048]{2,1,0:T(8,128)(2,1)S(1)}, bf16[1,128,2048]{2,1,0:T(8,128)(2,1)}, u32[]{:S(2)}) copy-start(bf16[1,128,2048]{2,1,0:T(8,128)(2,1)} %param.23) | copy-start | bytes 1572868
  7.2 254.5 %all-gather.3.cloned.1.call-start = ((), (), s32[]{:S(2)}) async-start(), calls=%async_computation.8 | async-start | bytes 34603008 | tf_op jit(solution)/shard_map/all_gather | solution.py:125
  39.0 54.1 %all-to-all-start = ((bf16[8,2,32768]{2,1,0:T(2,128)(2,1)}), bf16[8,2,32768]{2,1,0:T(2,128)(2,1)}, u32[]{:S(2)}, u32[]{:S(2)}) async-start(bf16[8,2,32768]{2,1,0:T(2,128)(2,1)} %reshape.234), calls=%async_computation | async-start | bytes 2097152 | tf_op jit(solution)/shard_map/all_to_all | solution.py:113
  93.1 46.7 %all-to-all-start.1 = ((bf16[8,2,32768]{2,1,0:T(2,128)(2,1)}), bf16[8,2,32768]{2,1,0:T(2,128)(2,1)}, u32[]{:S(2)}, u32[]{:S(2)}) async-start(bf16[8,2,32768]{2,1,0:T(2,128)(2,1)} %reshape.236), calls=%async_computation.1 | async-start | bytes 2097152 | tf_op jit(solution)/shard_map/all_to_all | solution.py:114
  100.6 30.7 %copy-start.14 = (s32[1,128]{1,0:T(1,128)S(1)}, s32[1,128]{1,0:T(1,128)}, u32[]{:S(2)}) copy-start(s32[1,128]{1,0:T(1,128)} %param.21) | copy-start | bytes 1540
  139.8 200.0 %all-to-all-start.2 = ((bf16[8,2,32768]{2,1,0:T(2,128)(2,1)}), bf16[8,2,32768]{2,1,0:T(2,128)(2,1)}, u32[]{:S(2)}, u32[]{:S(2)}) async-start(bf16[8,2,32768]{2,1,0:T(2,128)(2,1)} %reshape.238), calls=%async_computation.2 | async-start | bytes 2097152 | tf_op jit(solution)/shard_map/all_to_all | solution.py:115
  149.6 3.6 copy-start.5
  153.2 5.2 copy-start.10
  339.8 30.7 %all-to-all-start.4 = ((bf16[8,2,32768]{2,1,0:T(2,128)(2,1)}), bf16[8,2,32768]{2,1,0:T(2,128)(2,1)}, u32[]{:S(2)}, u32[]{:S(2)}) async-start(bf16[8,2,32768]{2,1,0:T(2,128)(2,1)} %reshape.242), calls=%async_computation.4 | async-start | bytes 2097152 | tf_op jit(solution)/shard_map/all_to_all | solution.py:136
  353.9 6.2 %copy-start.6 = (bf16[1024,4,128]{2,0,1:T(8,128)(2,1)S(1)}, bf16[1024,4,128]{2,0,1:T(8,128)(2,1)}, u32[]{:S(2)}) copy-start(bf16[1024,4,128]{2,0,1:T(8,128)(2,1)} %copy.132) | copy-start | bytes 3145732
  353.9 6.2 %copy-start.11 = (bf16[1024,4,128]{2,0,1:T(8,128)(2,1)S(1)}, bf16[1024,4,128]{2,0,1:T(8,128)(2,1)}, u32[]{:S(2)}) copy-start(bf16[1024,4,128]{2,0,1:T(8,128)(2,1)} %copy-done.10) | copy-start | bytes 3145732
  360.1 2.2 copy-start.2
  360.1 2.5 copy-start.13
  366.0 2.0 copy-start.8
  368.6 15.7 %copy-start.3 = (bf16[4,512,512]{1,2,0:T(8,128)(2,1)}, bf16[4,512,512]{1,2,0:T(8,128)(2,1)S(1)}, u32[]{:S(2)}) copy-start(bf16[4,512,512]{1,2,0:T(8,128)(2,1)S(1)} %fusion.15) | copy-start | bytes 6291460
  384.2 2.8 copy-start.9
  410.2 31.9 %all-to-all-start.3 = ((bf16[8,2,32768]{2,1,0:T(2,128)(2,1)}), bf16[8,2,32768]{2,1,0:T(2,128)(2,1)}, u32[]{:S(2)}, u32[]{:S(2)}) async-start(bf16[8,2,32768]{2,1,0:T(2,128)(2,1)} %reshape.240), calls=%async_computation.3 | async-start | bytes 2097152 | tf_op jit(solution)/shard_map/all_to_all | solution.py:122
  416.7 5.5 copy-start.7
  422.2 2.3 copy-start.12
  442.1 31.8 %all-to-all-start.6 = ((bf16[8,2,32768]{2,1,0:T(2,128)(2,1)}), bf16[8,2,32768]{2,1,0:T(2,128)(2,1)}, u32[]{:S(2)}, u32[]{:S(2)}) async-start(bf16[8,2,32768]{2,1,0:T(2,128)(2,1)} %reshape.246), calls=%async_computation.6 | async-start | bytes 2097152 | tf_op jit(solution)/shard_map/all_to_all | solution.py:145
  458.6 19.8 %copy-start.4 = (bf16[4,512,512]{1,2,0:T(8,128)(2,1)S(1)}, bf16[4,512,512]{1,2,0:T(8,128)(2,1)}, u32[]{:S(2)}) copy-start(bf16[4,512,512]{1,2,0:T(8,128)(2,1)} %copy-done.3) | copy-start | bytes 6291460
  473.9 44.1 %all-to-all-start.5 = ((bf16[8,2,32768]{2,1,0:T(2,128)(2,1)}), bf16[8,2,32768]{2,1,0:T(2,128)(2,1)}, u32[]{:S(2)}, u32[]{:S(2)}) async-start(bf16[8,2,32768]{2,1,0:T(2,128)(2,1)} %reshape.244), calls=%async_computation.5 | async-start | bytes 2097152 | tf_op jit(solution)/shard_map/all_to_all | solution.py:142
  518.0 34.6 %all-to-all-start.7 = ((bf16[8,2,32768]{2,1,0:T(2,128)(2,1)}), bf16[8,2,32768]{2,1,0:T(2,128)(2,1)}, u32[]{:S(2)}, u32[]{:S(2)}) async-start(bf16[8,2,32768]{2,1,0:T(2,128)(2,1)} %reshape.248), calls=%async_computation.7 | async-start | bytes 2097152 | tf_op jit(solution)/shard_map/all_to_all | solution.py:148
  552.6 8.6 %copy-start.1 = (bf16[1,128,2048]{2,1,0:T(8,128)(2,1)S(1)}, bf16[1,128,2048]{2,1,0:T(8,128)(2,1)}, u32[]{:S(2)}) copy-start(bf16[1,128,2048]{2,1,0:T(8,128)(2,1)} %param.23) | copy-start | bytes 1572868
Sparse Core Ops, SparseCore 0:
  11.0 250.6 all-gather.2
